TPU v7x, 32 devices: a whole 2x2x4 slice. The times are simulated.
32 devices in a mesh: row: 8 (over y, x, core), col: 4 (over z).
Axes of the slice: x: 2, y: 2, z: 4, core: 2. Of those that a mesh axis runs over, the one named last changes fastest.
Arguments:
- covariance: float32 [4096, 2, 2048], P('row', None, 'col'), may hold values from 0 to 1.1, as said below
- diag_inverse: float32 [512, 512], replicated, as said below
Outputs:
- panels: float32 [4096, 1024], P('row', 'col')
- trailing: float32 [4096, 2, 2048], P('row', None, 'col')
Inputs may be any that keep to these rules, and one draw needn't show every extreme that they name: `covariance`: K is symmetric and positive definite, its smallest eigenvalue 0.1 or more. `diag_inverse`: the inverse of the lower Cholesky factor of K[0:512, 0:512].
All inputs are finite; a program needn't handle non-finite values.
Results may differ from a plain program's by a relative error of at most 0.0003.
Values sent between devices are 32-bit elements; how exact they have to be, the bound alone decides.
No kernel may reach another device: no remote copies, remote signals or barrier semaphores. Data moves between devices by JAX's collectives and lax.ppermute only.
A program may use at most 128 MiB of HBM per device.

v0:
```python
import jax
import jax.numpy as jnp
from jax import lax
from jax.sharding import PartitionSpec as P

highest = lax.Precision.HIGHEST


def broadcast(array, axis, root):
    mine = lax.axis_index(axis) == root
    return lax.psum(jnp.where(mine, array, jnp.zeros_like(array)), axis)


def outer_product(left, right):
    return lax.dot_general(
        left, right, (((1,), (1,)), ((), ())), precision=highest, preferred_element_type=jnp.float32
    )


def local(covariance, diag_inverse):
    tile_size = covariance.shape[0]
    row_index = lax.axis_index("row")
    col_index = lax.axis_index("col")
    col_count = lax.axis_size("col")
    cycles = lax.axis_size("row") // col_count
    columns = [position * col_count + col_index for position in range(cycles)]
    block_tiles = [covariance[:, position, :] for position in range(cycles)]
    zero_tile = jnp.zeros((tile_size, tile_size), jnp.float32)
    local_first = lax.cond(
        col_index == 0, lambda: outer_product(block_tiles[0], diag_inverse), lambda: zero_tile
    )
    own_first = broadcast(local_first, "col", 0)
    slot_tiles = jnp.stack([jnp.where(row_index == column, own_first, 0.0) for column in columns])
    summed_first = lax.psum(slot_tiles, "row")
    remote_first = [summed_first[position] for position in range(cycles)]

    def lower_update(current, own_panel, remote_panel, column, first_col):
        keep_mask = (row_index >= column) & (column >= first_col)
        return lax.cond(
            keep_mask, lambda: current - outer_product(own_panel, remote_panel), lambda: current
        )

    block_tiles = [
        lower_update(block_tiles[position], own_first, remote_first[position], columns[position], 1)
        for position in range(cycles)
    ]
    is_owner = (row_index == 1) & (col_index == 1)
    identity = jnp.eye(tile_size, dtype=jnp.float32)
    factor_local = jnp.linalg.cholesky(jnp.where(is_owner, block_tiles[0], identity))
    factor = broadcast(factor_local, "row", 1)

    def solve_panel():
        solved = jax.scipy.linalg.solve_triangular(factor, block_tiles[0].T, lower=True).T
        return jnp.where(row_index >= 1, solved, 0.0)

    local_second = lax.cond(col_index == 1, solve_panel, lambda: zero_tile)
    own_second = broadcast(local_second, "col", 1)
    slot_second = jnp.stack([jnp.where(row_index == column, own_second, 0.0) for column in columns])
    summed_second = lax.psum(slot_second, "row")
    remote_second = [summed_second[position] for position in range(cycles)]
    block_tiles = [
        lower_update(
            block_tiles[position], own_second, remote_second[position], columns[position], 2
        )
        for position in range(cycles)
    ]
    finals = [
        jnp.where(
            (row_index >= columns[position]) & (columns[position] >= 2), block_tiles[position], 0.0
        )
        for position in range(cycles)
    ]
    trailing = jnp.stack(finals, axis=1)
    both_panels = jnp.concatenate([own_first, own_second], axis=1)
    share_width = both_panels.shape[1] // col_count
    panels = lax.dynamic_slice_in_dim(both_panels, col_index * share_width, share_width, 1)
    return (panels, trailing)


def solution(mesh):
    return jax.shard_map(
        local,
        mesh=mesh,
        in_specs=(P("row", None, "col"), P()),
        out_specs=(P("row", "col"), P("row", None, "col")),
        check_vma=False,
    )
```

profile of v0, /device:TPU:23, one launch (start us, length us, event | category | flops | bytes accessed | tf_op | source)
XLA Modules:
  0.0 480.2 jit_solution(18360229636380562185)
XLA Ops:
  7.2 5.0 %fusion.42 = (f32[512,1,512]{2,1,0:T(1,128)}, f32[512,1,512]{2,1,0:T(1,128)S(1)}) fusion(f32[512,2,512]{2,1,0:T(2,128)} %param.14), kind=kLoop, calls=%fused_computation.100 | loop fusion | bytes 4194304 | tf_op jit(solution)/shard_map/slice | solution.py:27
  14.7 51.8 %all-reduce.7.cloned.1.call-done = f32[512,512]{1,0:T(8,128)} async-done(((f32[512,512]{1,0:T(8,128)}), f32[512,512]{1,0:T(8,128)}) %all-reduce.7.cloned.1.call-update) | async-done | bytes 1048592 | tf_op jit(solution)/shard_map/psum | solution.py:11
  66.5 1.4 select_bitcast_fusion.5
  67.9 1.5 pad_maximum_fusion
  69.5 61.0 %all-reduce.9.cloned.1.call-done = f32[2,512,512]{2,1,0:T(8,128)} async-done(((f32[2,512,512]{2,1,0:T(8,128)}), f32[2,512,512]{2,1,0:T(8,128)}) %all-reduce.9.cloned.1.call-update) | async-done | bytes 2097168 | tf_op jit(solution)/shard_map/psum | solution.py:34
  130.6 3.5 conditional.7
  130.6 3.4 convolution_subtract_fusion
  135.6 2.5 copy.7
  138.1 1.5 fusion.28
  140.6 11.7 %cholesky.103 = f32[128,128]{1,0:T(8,128)S(1)} custom-call(f32[128,128]{1,0:T(8,128)S(1)} %cholesky.263), custom_call_target="Cholesky" | custom-call | tf_op jit(solution)/shard_map/jit(cholesky)/cholesky | solution.py:49
  152.3 9.8 %custom-call.31 = f32[1,128,128]{1,2,0:T(8,128)S(1)} custom-call(f32[1,128,128]{2,1,0:T(8,128)S(1)} %get-tuple-element.121), custom_call_target="InvertDiagBlocksLowerTriangular" | custom-call | tf_op jit(solution)/shard_map/jit(cholesky)/cholesky | solution.py:49
  162.3 1.2 constant_dynamic-update-slice_fusion.1
  163.5 1.3 convolution_subtract_fusion.7
  164.8 11.7 %cholesky.215 = f32[128,128]{1,0:T(8,128)S(1)} custom-call(f32[128,128]{1,0:T(8,128)S(1)} %cholesky.267), custom_call_target="Cholesky" | custom-call | tf_op jit(solution)/shard_map/jit(cholesky)/cholesky | solution.py:49
  176.5 10.0 %custom-call.32 = f32[1,128,128]{1,2,0:T(8,128)S(1)} custom-call(f32[1,128,128]{2,1,0:T(8,128)S(1)} %get-tuple-element.118), custom_call_target="InvertDiagBlocksLowerTriangular" | custom-call | tf_op jit(solution)/shard_map/jit(cholesky)/cholesky | solution.py:49
  186.8 1.3 convolution_subtract_fusion.8
  188.1 11.7 %cholesky.236 = f32[128,128]{1,0:T(8,128)S(1)} custom-call(f32[128,128]{1,0:T(8,128)S(1)} %cholesky.272), custom_call_target="Cholesky" | custom-call | tf_op jit(solution)/shard_map/jit(cholesky)/cholesky | solution.py:49
  200.5 9.8 %custom-call.33 = f32[1,128,128]{1,2,0:T(8,128)S(1)} custom-call(f32[1,128,128]{2,1,0:T(8,128)S(1)} %get-tuple-element.115), custom_call_target="InvertDiagBlocksLowerTriangular" | custom-call | tf_op jit(solution)/shard_map/jit(cholesky)/cholesky | solution.py:49
  211.7 12.1 %cholesky.253 = f32[128,128]{1,0:T(8,128)S(1)} custom-call(f32[128,128]{1,0:T(8,128)S(1)} %convolution_subtract_fusion.9), custom_call_target="Cholesky" | custom-call | tf_op jit(solution)/shard_map/jit(cholesky)/cholesky | solution.py:49
  229.0 55.6 %all-reduce.11.cloned.1.call-done = f32[512,512]{1,0:T(8,128)} async-done(((f32[512,512]{1,0:T(8,128)}), f32[512,512]{1,0:T(8,128)}) %all-reduce.11.cloned.1.call-update) | async-done | bytes 1048592 | tf_op jit(solution)/shard_map/psum | solution.py:11
  286.8 108.1 %all-reduce.13.cloned.1.call-done = f32[512,512]{1,0:T(8,128)} async-done(((f32[512,512]{1,0:T(8,128)}), f32[512,512]{1,0:T(8,128)}) %all-reduce.13.cloned.1.call-update) | async-done | bytes 1048592 | tf_op jit(solution)/shard_map/psum | solution.py:11
  395.0 1.5 select_bitcast_fusion.3
  396.5 1.5 pad_maximum_fusion.1
  400.2 4.5 conditional.10
  400.2 4.5 convolution_subtract_fusion.2
  405.6 53.2 %all-reduce.15.cloned.1.call-done = f32[2,512,512]{2,1,0:T(8,128)} async-done(((f32[2,512,512]{2,1,0:T(8,128)}), f32[2,512,512]{2,1,0:T(8,128)}) %all-reduce.15.cloned.1.call-update) | async-done | bytes 2097168 | tf_op jit(solution)/shard_map/psum | solution.py:59
  458.9 4.5 conditional.11
  459.0 4.4 convolution_subtract_fusion.3
  463.4 2.3 select_bitcast_fusion
  465.7 3.4 conditional.9
  465.7 3.4 convolution_subtract_fusion.1
  470.5 2.9 copy.10
  (50 shorter events, 18.1 us)
Async XLA Ops:
  7.2 59.4 %all-reduce.7.cloned.1.call-start = ((), (), s32[]{:S(2)}) async-start(), calls=%async_computation | async-start | bytes 2097152 | tf_op jit(solution)/shard_map/psum | solution.py:11
  12.2 1.2 copy-start.5
  14.7 115.9 %all-reduce.9.cloned.1.call-start = ((), (), s32[]{:S(2)}) async-start(), calls=%async_computation.1 | async-start | bytes 4194304 | tf_op jit(solution)/shard_map/psum | solution.py:34
  69.4 61.1 %copy-start = (f32[512,512]{1,0:T(8,128)S(1)}, f32[512,512]{1,0:T(8,128)}, u32[]{:S(2)}) copy-start(f32[512,512]{1,0:T(8,128)} %all-reduce.7.cloned.1.call-done) | copy-start | bytes 3145732
  69.5 215.1 %all-reduce.11.cloned.1.call-start = ((), (), s32[]{:S(2)}) async-start(), calls=%async_computation.2 | async-start | bytes 2097152 | tf_op jit(solution)/shard_map/psum | solution.py:11
  139.6 1.0 copy-start.4
  228.9 166.0 %all-reduce.13.cloned.1.call-start = ((), (), s32[]{:S(2)}) async-start(), calls=%async_computation.3 | async-start | bytes 2097152 | tf_op jit(solution)/shard_map/psum | solution.py:11
  286.8 172.1 %all-reduce.15.cloned.1.call-start = ((), (), s32[]{:S(2)}) async-start(), calls=%async_computation.4 | async-start | bytes 4194304 | tf_op jit(solution)/shard_map/psum | solution.py:59
  397.9 1.2 copy-start.3
  400.2 4.5 copy-start.1
  469.0 1.2 copy-start.2
Sparse Core Ops, SparseCore 0:
  14.8 51.7 all-reduce.6
  70.3 60.1 all-reduce.8
  229.1 55.4 all-reduce.10
  287.4 107.5 all-reduce.12
  398.6 60.1 all-reduce.14
where the time goes:
time: 487 us; the launch traced here: 480 us
  waiting for transfers between devices  330 us (68%)
  other arithmetic  94.2 us (19%)
  matrix products  21 us (4%)
  local copies, waits for them, and re-layouts  17.7 us (4%)
  between operations  16.8 us (3%)
    psum x3, waiting for transfers between devices, broadcast(): return lax.psum(jnp.where(mine, array, jnp.zeros_like(array)), axis)  216 us
    another operation x14, other arithmetic, local(): jnp.linalg.cholesky(jnp.where(is_owner, block_tiles[0], identity))  79 us
    psum x1, waiting for transfers between devices, local(): summed_first = lax.psum(slot_tiles, 'row')  61 us
    psum x1, waiting for transfers between devices, local(): summed_second = lax.psum(slot_second, 'row')  53.2 us
    dot_general x4, matrix products, outer_product(): lax.dot_general(left, right, (((1,), (1,)), ((), ())), precision=highest,...  15.6 us
  transfers between devices with their start and end apart: 5, of which 5 were waited for; matrix products, arithmetic and copies ran while one was open for 1% of the time, Pallas kernels for 0%

commit v1 on v0

v1 whole, which is shorter than its diff:
```python
import functools

import jax
import jax.numpy as jnp
from jax import lax
from jax.experimental import pallas as pl
from jax.experimental.pallas import tpu as pltpu
from jax.sharding import PartitionSpec as P

HIGHEST = lax.Precision.HIGHEST
AXES = ("row", "col")
SUB = 8


def dot(left, right, lhs_dim, rhs_dim):
    return lax.dot_general(
        left,
        right,
        (((lhs_dim,), (rhs_dim,)), ((), ())),
        precision=HIGHEST,
        preferred_element_type=jnp.float32,
    )


def nn(left, right):
    return dot(left, right, 1, 0)


def nt(left, right):
    return dot(left, right, 1, 1)


def tn(left, right):
    return dot(left, right, 0, 0)


def factor_block(work, aug, up):
    size = work.shape[0]
    groups = size // SUB
    rows = lax.broadcasted_iota(jnp.int32, (SUB, size), 0)
    lanes = lax.broadcasted_iota(jnp.int32, (SUB, size), 1)
    for t in range(groups):
        aug[t * SUB : (t + 1) * SUB, :] = jnp.where(lanes == rows + t * SUB, 1.0, 0.0)

    def lane(value, index):
        return jnp.broadcast_to(value[:, index : index + 1], (SUB, size))

    def row(value, index):
        return jnp.broadcast_to(value[index : index + 1, :], (SUB, size))

    for s in range(groups):
        here = slice(s * SUB, (s + 1) * SUB)
        own, own_aug = work[here, :], aug[here, :]
        columns = [lane(own, s * SUB + b) for b in range(SUB)]
        small = [[row(columns[b], a) if a >= b else None for b in range(SUB)] for a in range(SUB)]
        upper = [row(own, i) for i in range(SUB)]
        inverse = [row(own_aug, i) for i in range(SUB)]
        low = [[None] * SUB for _ in range(SUB)]
        scale = []
        for i in range(SUB):
            scale.append(lax.rsqrt(small[i][i]))
            for a in range(i + 1, SUB):
                low[a][i] = small[a][i] * scale[i]
            for b in range(i + 1, SUB):
                for a in range(b, SUB):
                    small[a][b] = small[a][b] - low[a][i] * low[b][i]
            upper[i] = upper[i] * scale[i]
            inverse[i] = inverse[i] * scale[i]
            for b in range(i + 1, SUB):
                upper[b] = upper[b] - upper[i] * low[b][i]
                inverse[b] = inverse[b] - inverse[i] * low[b][i]
        for t in range(s + 1, groups):
            there = slice(t * SUB, (t + 1) * SUB)
            current, current_aug = work[there, :], aug[there, :]
            part = [lane(current, s * SUB + b) for b in range(SUB)]
            for i in range(SUB):
                part[i] = part[i] * scale[i]
                for b in range(i + 1, SUB):
                    part[b] = part[b] - part[i] * low[b][i]
                current = current - part[i] * upper[i]
                current_aug = current_aug - part[i] * inverse[i]
            work[there, :] = current
            aug[there, :] = current_aug
        packed_inverse, packed_upper = inverse[0], upper[0]
        for i in range(1, SUB):
            packed_inverse = jnp.where(rows == i, inverse[i], packed_inverse)
            packed_upper = jnp.where(rows == i, upper[i], packed_upper)
        aug[here, :] = packed_inverse
        up[here, :] = jnp.where(lanes >= rows + s * SUB, packed_upper, 0.0)


def factor_pair(work, diag, aug, up, inv_ref, up_ref):
    size = work.shape[0]
    part = size // 2
    low, high = slice(0, part), slice(part, size)
    diag[...] = work[low, low]

    def step(k, carry):
        factor_block(diag, aug, up)

        @pl.when(k == 0)
        def _():
            inv = aug[...]
            cross = nn(inv, work[low, high])
            diag[...] = work[high, high] - tn(cross, cross)
            inv_ref[low, low] = inv
            inv_ref[low, high] = jnp.zeros_like(inv)
            up_ref[low, low] = up[...]
            up_ref[low, high] = cross

        @pl.when(k == 1)
        def _():
            inv = aug[...]
            inv_ref[high, high] = inv
            inv_ref[high, low] = -nn(inv, tn(up_ref[low, high], inv_ref[low, low]))
            up_ref[high, high] = up[...]
            up_ref[high, low] = jnp.zeros_like(inv)

        return carry

    lax.fori_loop(0, 2, step, 0)


def packed_of(inverse, upper):
    rows = lax.broadcasted_iota(jnp.int32, inverse.shape, 0)
    lanes = lax.broadcasted_iota(jnp.int32, inverse.shape, 1)
    return jnp.where(lanes <= rows, inverse, upper)


def lower_part(packed):
    rows = lax.broadcasted_iota(jnp.int32, packed.shape, 0)
    lanes = lax.broadcasted_iota(jnp.int32, packed.shape, 1)
    return jnp.where(lanes <= rows, packed, 0.0)


def factor_of(packed):
    rows = lax.broadcasted_iota(jnp.int32, packed.shape, 0)
    lanes = lax.broadcasted_iota(jnp.int32, packed.shape, 1)
    inverse_diag = jnp.where(lanes == rows, 1.0 / packed, 0.0)
    return jnp.where(lanes > rows, packed, inverse_diag).T


def place():
    return lax.axis_index("row"), lax.axis_index("col")


def fetch(target, semaphore, choices):
    for condition, source in choices:

        @pl.when(condition)
        def _(source=source):
            pltpu.make_async_copy(source, target, semaphore).start()

    return pltpu.make_async_copy(choices[0][1], target, semaphore).wait


def call(kernel, name, out_shapes, inputs, scratch, in_vmem=False, flops=0):
    outs = [jax.ShapeDtypeStruct(shape, jnp.float32) for shape in out_shapes]
    size = sum(4 * x.size for x in inputs) + sum(4 * x.size for x in outs)
    return pl.pallas_call(
        kernel,
        out_shape=outs,
        in_specs=[pl.BlockSpec(memory_space=pltpu.VMEM if in_vmem else pl.ANY)] * len(inputs),
        out_specs=[pl.BlockSpec(memory_space=pltpu.VMEM)] * len(outs),
        scratch_shapes=scratch,
        cost_estimate=pl.CostEstimate(flops=flops, bytes_accessed=size, transcendentals=0),
        name=name,
    )(*inputs)


def vmem(*shape):
    return pltpu.VMEM(shape, jnp.float32)


def copies(count):
    return pltpu.SemaphoreType.DMA((count,))


def split(refs, *counts):
    groups = []
    for count in counts:
        groups.append(refs[:count])
        refs = refs[count:]
    return groups


def extract_kernel(cov_ref, own_ref, low_ref, high_ref, *held_refs):
    half = low_ref.shape[0]
    cycles = cov_ref.shape[1]
    _, c = place()
    own = cov_ref[:, 0, :]
    own_ref[...] = own
    low_ref[...] = own[:half]
    high_ref[...] = own[half:]
    for t, held_ref in enumerate(held_refs):
        later = cov_ref[:, min(t + 1, cycles - 1), :]
        held_ref[...] = jnp.where(c < 2, later, cov_ref[:, t, :])


def factor_scratch(half):
    part = half // 2
    shapes = [(half, half), (part, part), (part, part), (part, part), (half, half), (half, half)]
    return [vmem(*shape) for shape in shapes]


def first_kernel(
    swapped_ref, own_ref, diag_ref, out_ref, rest_ref,
    corner, second, dinv, work, diag, aug, up, inv, upper, sems,
):
    half = out_ref.shape[0]
    r, c = place()
    owner = (r == 1) & (c == 1)

    @pl.when(owner)
    def _():
        waits = [
            fetch(corner, sems.at[0], [(owner, swapped_ref)]),
            fetch(dinv, sems.at[1], [(owner, diag_ref)]),
            fetch(second, sems.at[2], [(owner, own_ref)]),
        ]
        for wait in waits:
            wait()
        panel = nn(dinv[...], corner[...])
        second[...] = second[...] - tn(panel, panel)
        work[...] = second[:half, :half]
        factor_pair(work, diag, aug, up, inv, upper)
        cross = nn(inv[...], second[:half, half:])
        rest_ref[...] = second[half:, half:] - tn(cross, cross)
        out_ref[:, :half] = packed_of(inv[...], upper[...])
        out_ref[:, half:] = cross


def second_kernel(rest_ref, out_ref, work, diag, aug, up, inv, upper, sems):
    r, c = place()
    owner = (r == 1) & (c == 1)

    @pl.when(owner)
    def _():
        fetch(work, sems.at[0], [(owner, rest_ref)])()
        factor_pair(work, diag, aug, up, inv, upper)
        out_ref[...] = packed_of(inv[...], upper[...])


def early_kernel(cols, tiles, *refs):
    hops = cols - 1
    (own, back, diag), low, high, mine, other, held, (panel_ref, second_ref), first_t, part, rest = split(
        refs, 3, hops, hops, tiles, tiles, tiles, 2, tiles, tiles, 4
    )
    first, dinv, column, sems = rest
    half = low[0].shape[0]
    r, c = place()
    core = r % 2
    always = c >= 0
    waits = [fetch(dinv, sems.at[0], [(always, diag)])]
    for i, parts in enumerate((low, high)):
        rows = pl.ds(i * half, half)
        choices = [(c == 0, own.at[rows])]
        choices += [(c == b, parts[b - 1]) for b in range(1, cols)]
        waits.append(fetch(first.at[rows], sems.at[1 + i], choices))
        choices = [(c == 0, back.at[rows]), (c == 1, own.at[rows])]
        choices += [(c == b, parts[b - 2]) for b in range(2, cols)]
        waits.append(fetch(second_ref.at[rows], sems.at[3 + i], choices))
    for wait in waits:
        wait()
    panel_ref[...] = nt(first[...], dinv[...])
    for t in range(tiles):
        index = (t + jnp.where(c < 2, 1, 0)) * cols + c

        @pl.when(r >= index)
        def _(t=t):
            waits = [
                fetch(column, sems.at[5], [(core == 0, mine[t]), (core == 1, other[t])]),
                fetch(part[t], sems.at[6], [(always, held[t])]),
            ]
            for wait in waits:
                wait()
            first_t[t][...] = nn(dinv[...], column[...])
            part[t][...] = part[t][...] - nn(panel_ref[...], first_t[t][...])


def middle_kernel(cols, tiles, *refs):
    (even, odd, diag, panel, second), mine, other, first_t, (panel_ref, schur_ref), schur_t, rest = split(
        refs, 5, tiles, tiles, tiles, 2, tiles, 5
    )
    corner, dinv, corner_panel, column, sems = rest
    r, c = place()
    core = r % 2
    always = c >= 0
    waits = [
        fetch(dinv, sems.at[0], [(always, diag)]),
        fetch(corner, sems.at[1], [(core == 0, even), (core == 1, odd)]),
        fetch(panel_ref, sems.at[2], [(always, panel)]),
        fetch(schur_ref, sems.at[3], [(always, second)]),
    ]
    for wait in waits:
        wait()
    corner_panel[...] = nn(dinv[...], corner[...])

    @pl.when(r == 1)
    def _():
        panel_ref[...] = corner_panel[...].T

    schur_ref[...] = schur_ref[...] - nn(panel_ref[...], corner_panel[...])
    for t in range(tiles):
        index = (t + jnp.where(c < 2, 1, 0)) * cols + c

        @pl.when(r >= index)
        def _(t=t):
            waits = [
                fetch(column, sems.at[4], [(always, first_t[t])]),
                fetch(schur_t[t], sems.at[5], [(core == 1, mine[t]), (core == 0, other[t])]),
            ]
            for wait in waits:
                wait()
            schur_t[t][...] = schur_t[t][...] - tn(corner_panel[...], column[...])


def late_kernel(cols, cycles, tiles, *refs):
    (even0, odd0, even1, odd1, panel, schur, near_panel, near_schur, held), first_part, schur_t, outs, rest = split(
        refs, 9, tiles, tiles, 2, 9
    )
    panels_ref, trailing_ref = outs
    piece, corner, first, second, other, other_second, column, total, sems = rest
    half = corner.shape[0]
    low, high = slice(0, half), slice(half, 2 * half)
    r, c = place()
    core = r % 2
    always = c >= 0
    last = (cycles - 1) * cols + c
    near = (c >= 2) & (r // 2 == last // 2) & (r >= last)
    waits = [
        fetch(piece, sems.at[0], [(core == 0, even0), (core == 1, odd0)]),
        fetch(corner, sems.at[1], [(core == 0, even1), (core == 1, odd1)]),
        fetch(first, sems.at[2], [(always, panel)]),
        fetch(second, sems.at[3], [(always, schur)]),
    ]
    for wait in waits:
        wait()

    def solve(target):
        target[:, low] = nt(target[:, low], lower_part(piece[:, low]))
        update = target[:, high] - nn(target[:, low], piece[:, high])
        target[:, high] = nt(update, lower_part(corner[...]))

    solve(second)

    @pl.when(r == 0)
    def _():
        second[...] = jnp.zeros_like(second)

    @pl.when(r == 1)
    def _():
        second[low, low] = factor_of(piece[:, low])
        second[low, high] = jnp.zeros((half, half), jnp.float32)
        second[high, low] = piece[:, high].T
        second[high, high] = factor_of(corner[...])

    width = panels_ref.shape[1]
    for b in range(cols):

        @pl.when(c == b)
        def _(b=b):
            source, start = (first, b * width) if 2 * b < cols else (second, b * width - 2 * half)
            panels_ref[...] = source[:, start : start + width]

    trailing_ref[...] = jnp.zeros_like(trailing_ref)

    def store(t):
        for shift in (0, 1):
            if t + shift < cycles:

                @pl.when((c < 2) if shift else (c >= 2))
                def _(slot=t + shift):
                    trailing_ref[:, slot, :] = total[...]

    for t in range(tiles):
        index = (t + jnp.where(c < 2, 1, 0)) * cols + c
        wanted = r >= index
        if t + 1 == cycles:
            wanted = wanted & jnp.logical_not(near)

        @pl.when(wanted)
        def _(t=t):
            waits = [
                fetch(column, sems.at[4], [(always, schur_t[t])]),
                fetch(total, sems.at[5], [(always, first_part[t])]),
            ]
            for wait in waits:
                wait()
            column[low] = nn(lower_part(piece[:, low]), column[low])
            update = column[high] - tn(piece[:, high], column[low])
            column[high] = nn(lower_part(corner[...]), update)
            total[...] = total[...] - nn(second[...], column[...])
            store(t)

    @pl.when(near)
    def _():
        own = r == last
        waits = [
            fetch(other, sems.at[6], [(own, panel), (r != last, near_panel)]),
            fetch(other_second, sems.at[7], [(own, schur), (r != last, near_schur)]),
            fetch(total, sems.at[5], [(always, held)]),
        ]
        for wait in waits:
            wait()
        solve(other_second)
        value = total[...] - nt(first[...], other[...])
        total[...] = value - nt(second[...], other_second[...])
        store(cycles - 1)


def local(covariance, diag_inverse, rows, cols):
    tile = covariance.shape[0]
    cycles = covariance.shape[1]
    half = tile // 2
    chips = rows // 2
    r, c = place()
    chip, core = r // 2, r % 2
    whole = (tile, tile)

    def send(value, pairs):
        flat = [(a * cols + b, x * cols + y) for (a, b), (x, y) in pairs]
        return lax.ppermute(value, AXES, flat)

    bits = []
    while (1 << len(bits)) < chips:
        bits.append(1 << len(bits))

    def column_of(t, column):
        return (t + (1 if column < 2 else 0)) * cols + column

    own, own_low, own_high, *held = call(
        extract_kernel,
        "extract",
        [whole, (half, tile), (half, tile)] + [whole] * cycles,
        [covariance],
        [],
        in_vmem=True,
    )

    with jax.named_scope("swap"):
        swapped = send(own, [((0, 1), (1, 1))])

    def along(column, hop):
        pairs = []
        source = column - hop
        for a in range(rows):
            lead = a >= 2 and source in (0, 1)
            if lead or (a == 0 and (source == 1 or (source == 0 and hop == 0))):
                pairs.append(((a, column), (a, column + 1)))
        return pairs

    moved = []
    for name, part in (("low", own_low), ("high", own_high)):
        chain = []
        for hop in range(cols - 1):
            pairs = [pair for column in range(cols - 1) for pair in along(column, hop)]
            with jax.named_scope(f"along_{name}_{hop}"):
                part = send(part, pairs)
            chain.append(part)
        moved.append(chain)
    with jax.named_scope("back"):
        back = send(
            own, [((a, 1), (a, 0)) for a in range(rows) if a == 0 or a >= min(cols, rows - 1)]
        )

    def spread(value, wanted, cores, name):
        current = value
        for step in range(len(bits)):
            pairs = []
            arrived = False
            for k in cores:
                order = bits if k == 0 else bits[::-1]
                used, bit, later = sum(order[:step]), order[step], sum(order[step + 1 :])
                arrived = jnp.where(core == k, (chip & bit) != 0, arrived)
                for column in range(cols):
                    for q in range(chips):
                        target = q | bit
                        if q & ~used or target >= chips:
                            continue
                        reach = {target | extra for extra in range(chips) if not extra & ~later}
                        if reach & wanted(column):
                            pairs.append(((2 * q + k, column), (2 * target + k, column)))
            if pairs:
                with jax.named_scope(f"{name}_{step}"):
                    current = jnp.where(arrived, send(current, pairs), current)
        return current

    def trade(value, wanted, name, ways=(0, 1)):
        pairs = []
        for column in range(cols):
            for q in wanted(column):
                pairs += [((2 * q + k, column), (2 * q + 1 - k, column)) for k in ways]
        with jax.named_scope(name):
            return send(value, pairs)

    mine, other = [], []
    for t in range(cycles):

        def wanted(column, t=t):
            if column < 2 and t + 1 >= cycles:
                return set()
            edge = column_of(t, column) // 2 + (1 if t + 1 == cycles else 0)
            return {q for q in range(chips) if q >= edge and q > 0}

        if any(wanted(column) for column in range(cols)):
            mine.append(spread(held[t], wanted, (0, 1), f"column_{t}"))
            other.append(trade(mine[-1], wanted, f"column_trade_{t}"))
    tiles = len(mine)

    first_piece, remainder = call(
        first_kernel,
        "factor_first",
        [(half, tile), (half, half)],
        [swapped, own, diag_inverse],
        [vmem(*whole)] * 3 + factor_scratch(half) + [copies(3)],
    )
    second_piece = call(
        second_kernel,
        "factor_second",
        [(half, half)],
        [remainder],
        factor_scratch(half) + [copies(1)],
    )[0]

    def everyone(column):
        return set(range(chips))

    corner = jnp.where(c == 0, back, own)
    for b in range(2, cols):
        arrived = jnp.concatenate([moved[0][b - 2], moved[1][b - 2]], axis=0)
        corner = jnp.where(c == b, arrived, corner)
    corner = spread(corner, everyone, (0,), "corner")
    corner_odd = trade(corner, everyone, "corner_trade", (0,))

    def distribute(piece, name):
        current = piece
        for b in range(cols):
            if b != 1:
                with jax.named_scope(f"{name}_to_{b}"):
                    current = jnp.where(c == b, send(piece, [((1, 1), (1, b))]), current)
        current = spread(current, everyone, (1,), name)
        return current, trade(current, everyone, f"{name}_trade", (1,))

    first_odd, first_even = distribute(first_piece, "first_piece")
    second_odd, second_even = distribute(second_piece, "second_piece")

    product = 2 * tile**3
    panel, second, *products = call(
        functools.partial(early_kernel, cols, tiles),
        "early",
        [whole] * (2 + 2 * tiles),
        [own, back, diag_inverse, *moved[0], *moved[1], *mine, *other, *held[:tiles]],
        [vmem(*whole)] * 3 + [copies(7)],
        flops=3 * product,
    )
    first_t, partial = products[:tiles], products[tiles:]
    panel, schur, *schur_t = call(
        functools.partial(middle_kernel, cols, tiles),
        "middle",
        [whole] * (2 + tiles),
        [corner, corner_odd, diag_inverse, panel, second, *mine, *other, *first_t],
        [vmem(*whole)] * 4 + [copies(6)],
        flops=3 * product,
    )
    edges = [column_of(cycles - 1, b) for b in range(2, cols)]
    pairs = [((j, b), (j + 1, b)) for b, j in zip(range(2, cols), edges) if j % 2 == 0]
    with jax.named_scope("near_panel"):
        near_panel = send(panel, pairs)
    with jax.named_scope("near_schur"):
        near_schur = send(schur, pairs)
    panels, trailing = call(
        functools.partial(late_kernel, cols, cycles, tiles),
        "late",
        [(tile, 2 * tile // cols), covariance.shape],
        [
            first_even, first_odd, second_even, second_odd,
            panel, schur, near_panel, near_schur, held[-1], *partial, *schur_t,
        ],
        [vmem(half, tile), vmem(half, half)] + [vmem(*whole)] * 6 + [copies(8)],
        flops=4 * product,
    )
    return panels, trailing


def solution(mesh):
    rows, cols = mesh.shape["row"], mesh.shape["col"]
    return jax.shard_map(
        functools.partial(local, rows=rows, cols=cols),
        mesh=mesh,
        in_specs=(P("row", None, "col"), P()),
        out_specs=(P("row", "col"), P("row", None, "col")),
        check_vma=False,
    )
```

time: 487 us -> 188 us (0.39)
  waiting for transfers between devices: 330 us -> 52.1 us
  other arithmetic: 94.2 us -> 13 us
  Pallas kernels: 0 us -> 58.2 us
  starting transfers between devices: 0.2 us -> 57.6 us
  matrix products: 21 us -> 0 us
  between operations: 16.8 us -> 1.22 us
  local copies, waits for them, and re-layouts: 17.7 us -> 2.21 us
    psum x5 -> x0, waiting for transfers between devices: 330 us -> none  [the longest x3 216 us: broadcast(): return lax.psum(jnp.where(mine, array, jnp.zeros_like(array)), axis)]
    another operation x21 -> x0, other arithmetic: 87.5 us -> none  [the longest x14 79 us: local(): jnp.linalg.cholesky(jnp.where(is_owner, block_tiles[0], identity))]
    pallas_call x0 -> x6, Pallas kernels: none -> 58.2 us  [call(): pl.pallas_call(kernel, out_shape=outs, in_specs=[pl.BlockSpec(memory_spac...]
    ppermute x0 -> x28, starting transfers between devices: none -> 57.6 us  [send(): return lax.ppermute(value, AXES, flat)]
    ppermute x0 -> x28, waiting for transfers between devices: none -> 52.1 us  [send(): return lax.ppermute(value, AXES, flat)]
    dot_general x4 -> x0, matrix products: 15.6 us -> none  [outer_product(): lax.dot_general(left, right, (((1,), (1,)), ((), ())), precision=highest,...]
    select_n x4 -> x11, other arithmetic: 4.34 us -> 13 us  [the longest x8 7.58 us: spread(): current = jnp.where(arrived, send(current, pairs), current)]
    unnamed x15 -> x24, local copies, waits for them, and re-layouts: 8.48 us -> 2.21 us
  transfers between devices with their start and end apart: 5 -> 28, of which waited for: 5 -> 7; matrix products, arithmetic and copies ran while one was open for 1% -> 7% of each run, Pallas kernels for 0% -> 19%
where the time goes in v1:
time: 188 us; the launch traced here: 184 us
  Pallas kernels  58.2 us (31%)
  starting transfers between devices  57.6 us (31%)
  waiting for transfers between devices  52.1 us (28%)
  other arithmetic  13 us (7%)
  local copies, waits for them, and re-layouts  2.21 us (1%)
    pallas_call x6, Pallas kernels, call(): pl.pallas_call(kernel, out_shape=outs, in_specs=[pl.BlockSpec(memory_spac...  58.2 us
    ppermute x28, starting transfers between devices, send(): return lax.ppermute(value, AXES, flat)  57.6 us
    ppermute x28, waiting for transfers between devices, send(): return lax.ppermute(value, AXES, flat)  52.1 us
    select_n x8, other arithmetic, spread(): current = jnp.where(arrived, send(current, pairs), current)  7.58 us
  transfers between devices with their start and end apart: 28, of which 7 were waited for; matrix products, arithmetic and copies ran while one was open for 7% of the time, Pallas kernels for 19%

profile of v1, /device:TPU:23, one launch (start us, length us, event | category | flops | bytes accessed | tf_op | source)
XLA Modules:
  0.0 184.3 jit_solution(11890107791305153068)
XLA Ops:
  0.6 4.2 %extract.1 = (f32[512,512]{1,0:T(8,128)}, f32[256,512]{1,0:T(8,128)}, f32[256,512]{1,0:T(8,128)}, f32[512,512]{1,0:T(8,128)}, f32[512,512]{1,0:T(8,128)}) custom-call(f32[512,2,512]{2,1,0:T(2,128)} %cov_ref.1), custom_call_target="tpu_custom_call" | custom-call | bytes 6291456 | tf_op jit(solution)/shard_map/extract/pallas_call | solution.py:160
  8.1 12.4 %collective-permute-done.13.refs_3_ = f32[256,512]{1,0:T(8,128)S(1)} collective-permute-done((f32[256,512]{1,0:T(8,128)}, f32[256,512]{1,0:T(8,128)S(1)}, u32[]{:S(2)}, u32[]{:S(2)}) %collective-permute-start.13) | collective-permute-done | bytes 524320 | tf_op jit(solution)/shard_map/along_low_0/ppermute | solution.py:423
  20.6 1.9 %collective-permute-start.14 = (f32[256,512]{1,0:T(8,128)S(1)}, f32[256,512]{1,0:T(8,128)}, u32[]{:S(2)}, u32[]{:S(2)}) collective-permute-start(f32[256,512]{1,0:T(8,128)S(1)} %collective-permute-done.13.refs_3_), channel_id=1, source_target_pairs={{9,10},{13,14},{17,18},{21,22},{25,26},{29,30},{2,3},{10,11},{14,1... | collective-permute-start | bytes 1572872 | tf_op jit(solution)/shard_map/along_low_1/ppermute | solution.py:423
  22.5 9.3 %collective-permute-done.15.refs_6_ = f32[256,512]{1,0:T(8,128)S(1)} collective-permute-done((f32[256,512]{1,0:T(8,128)}, f32[256,512]{1,0:T(8,128)S(1)}, u32[]{:S(2)}, u32[]{:S(2)}) %collective-permute-start.15) | collective-permute-done | bytes 524320 | tf_op jit(solution)/shard_map/along_high_0/ppermute | solution.py:423
  31.8 1.9 %collective-permute-start.16 = (f32[256,512]{1,0:T(8,128)S(1)}, f32[256,512]{1,0:T(8,128)}, u32[]{:S(2)}, u32[]{:S(2)}) collective-permute-start(f32[256,512]{1,0:T(8,128)S(1)} %collective-permute-done.15.refs_6_), channel_id=1, source_target_pairs={{9,10},{13,14},{17,18},{21,22},{25,26},{29,30},{2,3},{10,11},{14,1... | collective-permute-start | bytes 1572872 | tf_op jit(solution)/shard_map/along_high_1/ppermute | solution.py:423
  33.7 1.7 collective-permute-start
  35.4 1.7 collective-permute-start.23
  37.0 6.1 %collective-permute-done.14.refs_4_ = f32[256,512]{1,0:T(8,128)} collective-permute-done((f32[256,512]{1,0:T(8,128)S(1)}, f32[256,512]{1,0:T(8,128)}, u32[]{:S(2)}, u32[]{:S(2)}) %collective-permute-start.14) | collective-permute-done | bytes 524320 | tf_op jit(solution)/shard_map/along_low_1/ppermute | solution.py:423
  43.1 11.2 %collective-permute-done.16.refs_7_ = f32[256,512]{1,0:T(8,128)} collective-permute-done((f32[256,512]{1,0:T(8,128)S(1)}, f32[256,512]{1,0:T(8,128)}, u32[]{:S(2)}, u32[]{:S(2)}) %collective-permute-start.16) | collective-permute-done | bytes 524320 | tf_op jit(solution)/shard_map/along_high_1/ppermute | solution.py:423
  54.4 2.0 %maximum_select_fusion = f32[512,512]{1,0:T(8,128)S(1)} fusion(f32[256,512]{1,0:T(8,128)} %collective-permute-done.16.refs_7_, f32[256,512]{1,0:T(8,128)} %collective-permute-done.14.refs_4_, f32[256,512]{1,0:T(8,128)S(1)} %collective-permute-done.15.refs_6_, f32[256,512]{1,0:T(8,128)S(1)} %collective-permute-done.13.refs_3_, ...), kind=kLoop, calls=%fused_computation | loop fusion | flops 1310720 | bytes 5242883 | tf_op jit(solution)/shard_map/jit(_where)/select_n | solution.py:532
  56.4 1.8 collective-permute-start.18
  59.1 1.5 collective-permute-start.1
  60.6 1.5 collective-permute-start.2
  62.1 1.4 broadcast_select_fusion
  64.8 1.5 collective-permute-start.3
  66.5 1.7 collective-permute-start.19
  68.2 2.2 %select_select_fusion = f32[256,512]{1,0:T(8,128)} fusion(f32[256,512]{1,0:T(8,128)} %collective-permute-done.1, f32[256,512]{1,0:T(8,128)} %collective-permute-done.2, f32[256,512]{1,0:T(8,128)} %collective-permute-done.3, f32[256,512]{1,0:T(8,128)} %get-tuple-element.17, pred[]{:T(512)S(6)} %eq.15, pred[]{:T(512)S(6)} %eq.14, pred[]{:T(512)S(6)} %eq.13), kind=kLoop, calls=%fused_computation.2 | loop fusion | flops 393216 | bytes 2621443 | tf_op jit(solution)/shard_map/first_piece_to_3/jit(_where)/select_n | solution.py:541
  70.4 1.4 collective-permute-start.4
  71.9 7.6 %collective-permute-done.24 = f32[512,512]{1,0:T(8,128)} collective-permute-done((f32[512,512]{1,0:T(8,128)S(1)}, f32[512,512]{1,0:T(8,128)}, u32[]{:S(2)}, u32[]{:S(2)}) %collective-permute-start.24) | collective-permute-done | bytes 1048608 | tf_op jit(solution)/shard_map/column_0_1/ppermute | solution.py:423
  79.4 1.4 broadcast_select_fusion.1.refs_9_.refs_5_
  80.9 4.3 %collective-permute-start.25 = (f32[512,512]{1,0:T(8,128)S(1)}, f32[512,512]{1,0:T(8,128)S(1)}, u32[]{:S(2)}, u32[]{:S(2)}) collective-permute-start(f32[512,512]{1,0:T(8,128)S(1)} %broadcast_select_fusion.1.refs_9_.refs_5_), channel_id=1, source_target_pairs={{16,20},{20,16},{24,28},{28,24},{17,21},{21,17},{25,29},{29,25},{1... | collective-permute-start | bytes 3145736 | tf_op jit(solution)/shard_map/column_trade_0/ppermute | solution.py:423
  88.5 1.4 collective-permute-start.7
  89.8 1.4 collective-permute-start.8
  91.2 1.3 collective-permute-start.21
  93.2 2.1 %collective-permute-start.22 = (f32[256,512]{1,0:T(8,128)}, f32[256,512]{1,0:T(8,128)}, u32[]{:S(2)}, u32[]{:S(2)}) collective-permute-start(f32[256,512]{1,0:T(8,128)} %collective-permute-done.16.refs_7_), channel_id=1, source_target_pairs={{10,11},{14,15},{18,19},{22,23},{26,27},{30,31}} | collective-permute-start | bytes 1572872 | tf_op jit(solution)/shard_map/along_high_2/ppermute | solution.py:423
  98.9 1.4 collective-permute-start.10
  100.3 4.2 %collective-permute-done.22.refs_8_ = f32[256,512]{1,0:T(8,128)} collective-permute-done((f32[256,512]{1,0:T(8,128)}, f32[256,512]{1,0:T(8,128)}, u32[]{:S(2)}, u32[]{:S(2)}) %collective-permute-start.22) | collective-permute-done | bytes 524320 | tf_op jit(solution)/shard_map/along_high_2/ppermute | solution.py:423
  105.5 22.8 %early.1 = (f32[512,512]{1,0:T(8,128)}, f32[512,512]{1,0:T(8,128)}, f32[512,512]{1,0:T(8,128)}, f32[512,512]{1,0:T(8,128)}) custom-call(f32[512,512]{1,0:T(8,128)} %get-tuple-element.16.own_ref.refs_0_, f32[512,512]{1,0:T(8,128)} %copy-done.2, f32[512,512]{1,0:T(8,128)} %refs_2_.3, f32[256,512]{1,0:T(8,128)} %copy-done.4, ...), custom_call_target="tpu_custom_call" | custom-call | flops 805306368 | bytes 13631488 | tf_op jit(solution)/shard_map/early/pallas_call | solution.py:160
  128.3 11.0 %middle.1 = (f32[512,512]{1,0:T(8,128)}, f32[512,512]{1,0:T(8,128)}, f32[512,512]{1,0:T(8,128)}) custom-call(f32[512,512]{1,0:T(8,128)} %broadcast_select_fusion.3.refs_0_, f32[512,512]{1,0:T(8,128)} %collective-permute-done.20.refs_1_, f32[512,512]{1,0:T(8,128)} %refs_2_.3, f32[512,512]{1,0:T(8,128)} %get-tuple-element.22.refs_3_, ...), custom_call_target="tpu_custom_call" | custom-call | flops 805306368 | bytes 11534336 | tf_op jit(solution)/shard_map/middle/pallas_call | solution.py:160
  145.5 16.3 %collective-permute-start.6 = (f32[256,512]{1,0:T(8,128)S(1)}, f32[256,512]{1,0:T(8,128)S(1)}, u32[]{:S(2)}, u32[]{:S(2)}) collective-permute-start(f32[256,512]{1,0:T(8,128)S(1)} %broadcast_select_fusion.5.refs_1_), channel_id=1, source_target_pairs={{4,0},{12,8},{20,16},{28,24},{5,1},{13,9},{21,17},{29,25},{6,2},{1... | collective-permute-start | bytes 1572872 | tf_op jit(solution)/shard_map/first_piece_trade/ppermute | solution.py:423
  161.9 1.3 collective-permute-start.12
  165.6 18.6 %late.1 = (f32[512,256]{1,0:T(8,128)}, f32[512,2,512]{2,1,0:T(2,128)}) custom-call(f32[256,512]{1,0:T(8,128)} %copy-done.10, f32[256,512]{1,0:T(8,128)} %copy-done.6, f32[256,256]{1,0:T(8,128)} %copy-done.11, f32[256,256]{1,0:T(8,128)} %copy-done.8, f32[512,512]{1,0:T(8,128)} %get-tuple-element.25.refs_4_, f32[512,512]{1,0:T(8,128)} %get-tuple-element.26.refs_5_, ...), custom_call_target="tpu_custom_call" | custom-call | flops 1073741824 | bytes 11534336 | tf_op jit(solution)/shard_map/late/pallas_call | solution.py:160
  (65 shorter events, 22.6 us)
Async XLA Ops:
  4.8 32.2 %collective-permute-start.17 = (f32[512,512]{1,0:T(8,128)}, f32[512,512]{1,0:T(8,128)S(1)}, u32[]{:S(2)}, u32[]{:S(2)}) collective-permute-start(f32[512,512]{1,0:T(8,128)} %get-tuple-element.16.own_ref.refs_0_), channel_id=1, source_target_pairs={{1,0},{17,16},{21,20},{25,24},{29,28}} | collective-permute-start | bytes 3145736 | tf_op jit(solution)/shard_map/back/ppermute | solution.py:423
  5.5 15.0 %collective-permute-start.13 = (f32[256,512]{1,0:T(8,128)}, f32[256,512]{1,0:T(8,128)S(1)}, u32[]{:S(2)}, u32[]{:S(2)}) collective-permute-start(f32[256,512]{1,0:T(8,128)} %get-tuple-element.19), channel_id=1, source_target_pairs={{0,1},{8,9},{12,13},{16,17},{20,21},{24,25},{28,29},{1,2},{9,10},{... | collective-permute-start | bytes 1572872 | tf_op jit(solution)/shard_map/along_low_0/ppermute | solution.py:423
  6.8 25.0 %collective-permute-start.15 = (f32[256,512]{1,0:T(8,128)}, f32[256,512]{1,0:T(8,128)S(1)}, u32[]{:S(2)}, u32[]{:S(2)}) collective-permute-start(f32[256,512]{1,0:T(8,128)} %get-tuple-element.20), channel_id=1, source_target_pairs={{0,1},{8,9},{12,13},{16,17},{20,21},{24,25},{28,29},{1,2},{9,10},{... | collective-permute-start | bytes 1572872 | tf_op jit(solution)/shard_map/along_high_0/ppermute | solution.py:423
  20.6 33.8 %copy-start.4 = (f32[256,512]{1,0:T(8,128)}, f32[256,512]{1,0:T(8,128)S(1)}, u32[]{:S(2)}) copy-start(f32[256,512]{1,0:T(8,128)S(1)} %collective-permute-done.13.refs_3_) | copy-start | bytes 1572868
  20.6 22.6 %collective-permute-start.14 = (f32[256,512]{1,0:T(8,128)S(1)}, f32[256,512]{1,0:T(8,128)}, u32[]{:S(2)}, u32[]{:S(2)}) collective-permute-start(f32[256,512]{1,0:T(8,128)S(1)} %collective-permute-done.13.refs_3_), channel_id=1, source_target_pairs={{9,10},{13,14},{17,18},{21,22},{25,26},{29,30},{2,3},{10,11},{14,1... | collective-permute-start | bytes 1572872 | tf_op jit(solution)/shard_map/along_low_1/ppermute | solution.py:423
  31.8 22.6 %copy-start.5 = (f32[256,512]{1,0:T(8,128)}, f32[256,512]{1,0:T(8,128)S(1)}, u32[]{:S(2)}) copy-start(f32[256,512]{1,0:T(8,128)S(1)} %collective-permute-done.15.refs_6_) | copy-start | bytes 1572868
  31.8 22.6 %collective-permute-start.16 = (f32[256,512]{1,0:T(8,128)S(1)}, f32[256,512]{1,0:T(8,128)}, u32[]{:S(2)}, u32[]{:S(2)}) collective-permute-start(f32[256,512]{1,0:T(8,128)S(1)} %collective-permute-done.15.refs_6_), channel_id=1, source_target_pairs={{9,10},{13,14},{17,18},{21,22},{25,26},{29,30},{2,3},{10,11},{14,1... | collective-permute-start | bytes 1572872 | tf_op jit(solution)/shard_map/along_high_1/ppermute | solution.py:423
  33.7 24.5 %collective-permute-start = (f32[512,512]{1,0:T(8,128)}, f32[512,512]{1,0:T(8,128)}, u32[]{:S(2)}, u32[]{:S(2)}) collective-permute-start(f32[512,512]{1,0:T(8,128)} %get-tuple-element.16.own_ref.refs_0_), channel_id=1, source_target_pairs={{1,5}} | collective-permute-start | bytes 3145736 | tf_op jit(solution)/shard_map/swap/ppermute | solution.py:423
  35.4 26.7 %collective-permute-start.23 = (f32[512,512]{1,0:T(8,128)}, f32[512,512]{1,0:T(8,128)}, u32[]{:S(2)}, u32[]{:S(2)}) collective-permute-start(f32[512,512]{1,0:T(8,128)} %get-tuple-element.21.refs_11_), channel_id=1, source_target_pairs={{0,8},{1,9},{2,10},{3,11},{4,20},{5,21},{6,22},{7,23}} | collective-permute-start | bytes 3145736 | tf_op jit(solution)/shard_map/column_0_0/ppermute | solution.py:423
  37.0 19.4 %copy-start.2 = (f32[512,512]{1,0:T(8,128)}, f32[512,512]{1,0:T(8,128)S(1)}, u32[]{:S(2)}) copy-start(f32[512,512]{1,0:T(8,128)S(1)} %collective-permute-done.17.refs_1_) | copy-start | bytes 3145732
  56.4 9.9 %collective-permute-start.18 = (f32[512,512]{1,0:T(8,128)S(1)}, f32[512,512]{1,0:T(8,128)}, u32[]{:S(2)}, u32[]{:S(2)}) collective-permute-start(f32[512,512]{1,0:T(8,128)S(1)} %maximum_select_fusion), channel_id=1, source_target_pairs={{0,8},{1,9},{2,10},{3,11}} | collective-permute-start | bytes 3145736 | tf_op jit(solution)/shard_map/corner_0/ppermute | solution.py:423
  59.1 9.1 %collective-permute-start.1 = (f32[256,512]{1,0:T(8,128)}, f32[256,512]{1,0:T(8,128)}, u32[]{:S(2)}, u32[]{:S(2)}) collective-permute-start(f32[256,512]{1,0:T(8,128)} %get-tuple-element.17), channel_id=1, source_target_pairs={{5,7}} | collective-permute-start | bytes 1572872 | tf_op jit(solution)/shard_map/first_piece_to_3/ppermute | solution.py:423
  60.6 7.6 %collective-permute-start.2 = (f32[256,512]{1,0:T(8,128)}, f32[256,512]{1,0:T(8,128)}, u32[]{:S(2)}, u32[]{:S(2)}) collective-permute-start(f32[256,512]{1,0:T(8,128)} %get-tuple-element.17), channel_id=1, source_target_pairs={{5,6}} | collective-permute-start | bytes 1572872 | tf_op jit(solution)/shard_map/first_piece_to_2/ppermute | solution.py:423
  63.5 15.9 %collective-permute-start.24 = (f32[512,512]{1,0:T(8,128)S(1)}, f32[512,512]{1,0:T(8,128)}, u32[]{:S(2)}, u32[]{:S(2)}) collective-permute-start(f32[512,512]{1,0:T(8,128)S(1)} %broadcast_select_fusion), channel_id=1, source_target_pairs={{0,16},{8,24},{1,17},{9,25},{2,18},{10,26},{3,19},{11,27},{20,28},... | collective-permute-start | bytes 3145736 | tf_op jit(solution)/shard_map/column_0_1/ppermute | solution.py:423
  64.8 3.4 %collective-permute-start.3 = (f32[256,512]{1,0:T(8,128)}, f32[256,512]{1,0:T(8,128)}, u32[]{:S(2)}, u32[]{:S(2)}) collective-permute-start(f32[256,512]{1,0:T(8,128)} %get-tuple-element.17), channel_id=1, source_target_pairs={{5,4}} | collective-permute-start | bytes 1572872 | tf_op jit(solution)/shard_map/first_piece_to_0/ppermute | solution.py:423
  66.5 18.7 %collective-permute-start.19 = (f32[512,512]{1,0:T(8,128)S(1)}, f32[512,512]{1,0:T(8,128)}, u32[]{:S(2)}, u32[]{:S(2)}) collective-permute-start(f32[512,512]{1,0:T(8,128)S(1)} %broadcast_select_fusion.2), channel_id=1, source_target_pairs={{0,16},{8,24},{1,17},{9,25},{2,18},{10,26},{3,19},{11,27}} | collective-permute-start | bytes 3145736 | tf_op jit(solution)/shard_map/corner_1/ppermute | solution.py:423
  70.4 22.8 %collective-permute-start.4 = (f32[256,512]{1,0:T(8,128)}, f32[256,512]{1,0:T(8,128)}, u32[]{:S(2)}, u32[]{:S(2)}) collective-permute-start(f32[256,512]{1,0:T(8,128)} %select_select_fusion), channel_id=1, source_target_pairs={{4,20},{5,21},{6,22},{7,23}} | collective-permute-start | bytes 1572872 | tf_op jit(solution)/shard_map/first_piece_0/ppermute | solution.py:423
  80.9 23.6 %collective-permute-start.25 = (f32[512,512]{1,0:T(8,128)S(1)}, f32[512,512]{1,0:T(8,128)S(1)}, u32[]{:S(2)}, u32[]{:S(2)}) collective-permute-start(f32[512,512]{1,0:T(8,128)S(1)} %broadcast_select_fusion.1.refs_9_.refs_5_), channel_id=1, source_target_pairs={{16,20},{20,16},{24,28},{28,24},{17,21},{21,17},{25,29},{29,25},{1... | collective-permute-start | bytes 3145736 | tf_op jit(solution)/shard_map/column_trade_0/ppermute | solution.py:423
  86.4 41.9 %collective-permute-start.20 = (f32[512,512]{1,0:T(8,128)}, f32[512,512]{1,0:T(8,128)}, u32[]{:S(2)}, u32[]{:S(2)}) collective-permute-start(f32[512,512]{1,0:T(8,128)} %broadcast_select_fusion.3.refs_0_), channel_id=1, source_target_pairs={{0,4},{8,12},{16,20},{24,28},{1,5},{9,13},{17,21},{25,29},{2,6},{1... | collective-permute-start | bytes 3145736 | tf_op jit(solution)/shard_map/corner_trade/ppermute | solution.py:423
  88.5 2.7 %collective-permute-start.7 = (f32[256,256]{1,0:T(8,128)}, f32[256,256]{1,0:T(8,128)}, u32[]{:S(2)}, u32[]{:S(2)}) collective-permute-start(f32[256,256]{1,0:T(8,128)} %factor_second.1), channel_id=1, source_target_pairs={{5,7}} | collective-permute-start | bytes 786440 | tf_op jit(solution)/shard_map/second_piece_to_3/ppermute | solution.py:423
  89.8 2.7 %collective-permute-start.8 = (f32[256,256]{1,0:T(8,128)}, f32[256,256]{1,0:T(8,128)}, u32[]{:S(2)}, u32[]{:S(2)}) collective-permute-start(f32[256,256]{1,0:T(8,128)} %factor_second.1), channel_id=1, source_target_pairs={{5,6}} | collective-permute-start | bytes 786440 | tf_op jit(solution)/shard_map/second_piece_to_2/ppermute | solution.py:423
  91.2 7.7 %collective-permute-start.21 = (f32[256,512]{1,0:T(8,128)}, f32[256,512]{1,0:T(8,128)S(1)}, u32[]{:S(2)}, u32[]{:S(2)}) collective-permute-start(f32[256,512]{1,0:T(8,128)} %collective-permute-done.14.refs_4_), channel_id=1, source_target_pairs={{10,11},{14,15},{18,19},{22,23},{26,27},{30,31}} | collective-permute-start | bytes 1572872 | tf_op jit(solution)/shard_map/along_low_2/ppermute | solution.py:423
  92.5 3.9 %collective-permute-start.9 = (f32[256,256]{1,0:T(8,128)}, f32[256,256]{1,0:T(8,128)S(1)}, u32[]{:S(2)}, u32[]{:S(2)}) collective-permute-start(f32[256,256]{1,0:T(8,128)} %factor_second.1), channel_id=1, source_target_pairs={{5,4}} | collective-permute-start | bytes 786440 | tf_op jit(solution)/shard_map/second_piece_to_0/ppermute | solution.py:423
  93.2 11.3 %collective-permute-start.22 = (f32[256,512]{1,0:T(8,128)}, f32[256,512]{1,0:T(8,128)}, u32[]{:S(2)}, u32[]{:S(2)}) collective-permute-start(f32[256,512]{1,0:T(8,128)} %collective-permute-done.16.refs_7_), channel_id=1, source_target_pairs={{10,11},{14,15},{18,19},{22,23},{26,27},{30,31}} | collective-permute-start | bytes 1572872 | tf_op jit(solution)/shard_map/along_high_2/ppermute | solution.py:423
  96.5 47.8 %collective-permute-start.5 = (f32[256,512]{1,0:T(8,128)S(1)}, f32[256,512]{1,0:T(8,128)}, u32[]{:S(2)}, u32[]{:S(2)}) collective-permute-start(f32[256,512]{1,0:T(8,128)S(1)} %broadcast_select_fusion.4), channel_id=1, source_target_pairs={{4,12},{20,28},{5,13},{21,29},{6,14},{22,30},{7,15},{23,31}} | collective-permute-start | bytes 1572872 | tf_op jit(solution)/shard_map/first_piece_1/ppermute | solution.py:423
  98.9 43.1 %collective-permute-start.10 = (f32[256,256]{1,0:T(8,128)S(1)}, f32[256,256]{1,0:T(8,128)}, u32[]{:S(2)}, u32[]{:S(2)}) collective-permute-start(f32[256,256]{1,0:T(8,128)S(1)} %select_select_fusion.1), channel_id=1, source_target_pairs={{4,20},{5,21},{6,22},{7,23}} | collective-permute-start | bytes 786440 | tf_op jit(solution)/shard_map/second_piece_0/ppermute | solution.py:423
  139.4 24.9 %collective-permute-start.26 = (f32[512,512]{1,0:T(8,128)}, f32[512,512]{1,0:T(8,128)S(1)}, u32[]{:S(2)}, u32[]{:S(2)}) collective-permute-start(f32[512,512]{1,0:T(8,128)} %get-tuple-element.25.refs_4_), channel_id=1, source_target_pairs={{26,30}} | collective-permute-start | bytes 3145736 | tf_op jit(solution)/shard_map/near_panel/ppermute | solution.py:423
  140.7 23.6 %collective-permute-start.27 = (f32[512,512]{1,0:T(8,128)}, f32[512,512]{1,0:T(8,128)}, u32[]{:S(2)}, u32[]{:S(2)}) collective-permute-start(f32[512,512]{1,0:T(8,128)} %get-tuple-element.26.refs_5_), channel_id=1, source_target_pairs={{26,30}} | collective-permute-start | bytes 3145736 | tf_op jit(solution)/shard_map/near_schur/ppermute | solution.py:423
  143.0 18.8 %collective-permute-start.11 = (f32[256,256]{1,0:T(8,128)S(1)}, f32[256,256]{1,0:T(8,128)S(1)}, u32[]{:S(2)}, u32[]{:S(2)}) collective-permute-start(f32[256,256]{1,0:T(8,128)S(1)} %broadcast_select_fusion.6), channel_id=1, source_target_pairs={{4,12},{20,28},{5,13},{21,29},{6,14},{22,30},{7,15},{23,31}} | collective-permute-start | bytes 786440 | tf_op jit(solution)/shard_map/second_piece_1/ppermute | solution.py:423
  145.5 18.9 %copy-start.6 = (f32[256,512]{1,0:T(8,128)}, f32[256,512]{1,0:T(8,128)S(1)}, u32[]{:S(2)}) copy-start(f32[256,512]{1,0:T(8,128)S(1)} %broadcast_select_fusion.5.refs_1_) | copy-start | bytes 1572868
  145.5 18.8 %collective-permute-start.6 = (f32[256,512]{1,0:T(8,128)S(1)}, f32[256,512]{1,0:T(8,128)S(1)}, u32[]{:S(2)}, u32[]{:S(2)}) collective-permute-start(f32[256,512]{1,0:T(8,128)S(1)} %broadcast_select_fusion.5.refs_1_), channel_id=1, source_target_pairs={{4,0},{12,8},{20,16},{28,24},{5,1},{13,9},{21,17},{29,25},{6,2},{1... | collective-permute-start | bytes 1572872 | tf_op jit(solution)/shard_map/first_piece_trade/ppermute | solution.py:423
  161.9 2.4 %collective-permute-start.12 = (f32[256,256]{1,0:T(8,128)S(1)}, f32[256,256]{1,0:T(8,128)S(1)}, u32[]{:S(2)}, u32[]{:S(2)}) collective-permute-start(f32[256,256]{1,0:T(8,128)S(1)} %broadcast_select_fusion.7.refs_3_), channel_id=1, source_target_pairs={{4,0},{12,8},{20,16},{28,24},{5,1},{13,9},{21,17},{29,25},{6,2},{1... | collective-permute-start | bytes 786440 | tf_op jit(solution)/shard_map/second_piece_trade/ppermute | solution.py:423
  (8 other events, 33.2 us)
